TPU v7x, 128 devices: a whole 4x4x4 slice. The times are simulated.
128 devices in a mesh: seq: 32 (over y, z, core), head: 4 (over x).
Axes of the slice: x: 4, y: 4, z: 4, core: 2. Of those that a mesh axis runs over, the one named last changes fastest.
Arguments:
- image_patches: bfloat16 [32, 256, 1152], P('seq', None, 'head'), may hold values from -6 to 6
- text_embed: bfloat16 [8192, 2048], P('seq', 'head'), may hold values from -6 to 6
- image_start: int32 [32], replicated, may hold values from 0 to 126, as said below
- image_forget: float32 [32], replicated, may hold values from 0.001 to 0.3
- adapter: bfloat16 [1152, 2048], P('head'), may hold values from -0.1875 to 0.1875
- norm_gain: float32 [2048], replicated, may hold values from 0.5 to 1.5
- in_proj: bfloat16 [2048, 4, 2048], P(None, None, 'head'), may hold values from -0.125 to 0.125
- decay_proj: bfloat16 [2048, 16], P(None, 'head'), may hold values from -0.125 to 0.125
- head_decay_ceiling: float32 [16], P('head'), may hold values from 0 to 1, as said below
- out_gain: float32 [16, 128], P('head'), may hold values from 0.5 to 1.5
- out_proj: bfloat16 [2048, 2048], P('head'), may hold values from -0.125 to 0.125
Outputs:
- image_out: bfloat16 [32, 256, 2048], P('seq', None, 'head')
- text_out: bfloat16 [8192, 2048], P('seq', 'head')
Inputs may be any that keep to these rules, and one draw needn't show every extreme that they name: `image_start`: each entry is even; the images take distinct pairs of blocks. The merged piece of 512 tokens on one device of seq never holds both the image and the text that one device of seq holds in the source layout. `head_decay_ceiling`: Positive.
All inputs are finite; a program needn't handle non-finite values.
Results may differ from a plain program's by a relative error of at most 0.0095.
Values may be sent and summed in bfloat16 or wider, within the bound.
No kernel may reach another device: no remote copies, remote signals or barrier semaphores. Data moves between devices by JAX's collectives and lax.ppermute only.
A program may use at most 128 MiB of HBM per device.

v0:
```python
import jax
import jax.numpy as jnp
from jax import lax
from jax.sharding import Mesh
from jax.sharding import PartitionSpec as P

SEQ = ("seq_0", "seq_1", "seq_2")
EPSILON = 1e-06


def split_up(array, dim, length):
    shape = array.shape
    pieces = array.reshape(*shape[:dim], length, shape[dim] // length, *shape[dim + 1 :])
    return jnp.moveaxis(pieces, dim, 0)


def sent_and_summed(array, axis, dim):
    pieces = split_up(array, dim, lax.axis_size(axis))
    arrived = lax.all_to_all(pieces, axis, split_axis=0, concat_axis=0, tiled=True)
    return arrived.sum(axis=0)


def in_order(pieces, dim):
    shape = list(pieces.shape[1:])
    shape[dim] *= pieces.shape[0]
    return jnp.moveaxis(pieces, 0, dim).reshape(shape)


def copy_for_each(array, axis):
    length = lax.axis_size(axis)
    return lax.all_to_all(
        jnp.broadcast_to(array[None], (length, *array.shape)), axis, 0, 0, tiled=True
    )


def gathered_copies(array, axis, dim):
    return in_order(copy_for_each(array, axis), dim)


def neutral_like(array, identity):
    return jax.tree.map(
        lambda a, e: jnp.broadcast_to(jnp.asarray(e, a.dtype), a.shape), array, identity
    )


def entering_2(array, axes, combine, identity):
    before = start = neutral_like(array, identity)
    total = array
    for axis in reversed(axes):
        length, position = (lax.axis_size(axis), lax.axis_index(axis))
        pieces = jax.tree.map(
            lambda part, kind: lax.all_gather(part.astype(kind), axis),
            total,
            (jnp.bfloat16, jnp.bfloat16),
        )
        inside, total = (start, start)
        for k in range(length):
            passed = k < position
            total = combine(
                total, jax.tree.map(lambda part, own: part[k].astype(own.dtype), pieces, array)
            )
            inside = jax.tree.map(lambda new, old: jnp.where(passed, new, old), total, inside)
        before = combine(inside, before)
    return before


def sent_and_summed_2(array, axis, dim):
    pieces = split_up(array, dim, lax.axis_size(axis))
    arrived = lax.all_to_all(pieces, axis, split_axis=0, concat_axis=0, tiled=True)
    return arrived.astype(jnp.float32).sum(axis=0)


def rms_scale(values, gain_row):
    mean_square = jnp.mean(values * values, axis=-1, keepdims=True)
    return values * lax.rsqrt(mean_square + EPSILON) * gain_row


def shards(
    image_patches,
    text_embed,
    image_start,
    image_forget,
    adapter,
    norm_gain,
    in_proj,
    decay_proj,
    head_decay_ceiling,
    out_gain,
    out_proj,
):
    seq_count = lax.axis_size(SEQ)
    my_index = lax.axis_index(SEQ)
    patch_row_block = text_embed.shape[0]
    local_width = text_embed.shape[1]
    share_rows = patch_row_block // seq_count
    unit_count = 2 * seq_count
    token_rows = 2 * patch_row_block
    unit_ids = jnp.arange(unit_count, dtype=jnp.int32)
    device_ids = jnp.arange(seq_count, dtype=jnp.int32)
    unit_of_image = image_start // 2
    image_hits = (unit_of_image[:, None] == unit_ids[None, :]).astype(jnp.int32)
    is_image = jnp.sum(image_hits, axis=0)
    image_here = jnp.sum(image_hits * device_ids[:, None], axis=0)
    is_text = 1 - is_image
    text_here = jnp.cumsum(is_text) - is_text
    text_pick = ((is_text[None, :] == 1) & (text_here[None, :] == device_ids[:, None])).astype(
        jnp.int32
    )
    text_unit = jnp.sum(text_pick * unit_ids[None, :], axis=1)
    source = jnp.where(is_image == 1, image_here, text_here)
    my_units = 2 * my_index + jnp.arange(2, dtype=jnp.int32)
    unit_image = jnp.take(is_image, my_units)
    partial_value = jnp.dot(image_patches[0], adapter, preferred_element_type=jnp.float32)
    embedded = sent_and_summed(partial_value, "head", 1).astype(jnp.bfloat16)
    units_here = jnp.stack([embedded, text_embed]).reshape(2, seq_count, share_rows, local_width)
    spread = lax.all_to_all(units_here, SEQ, split_axis=1, concat_axis=1, tiled=True)
    table = spread.reshape(unit_count, share_rows, local_width)
    pick_index = is_text * seq_count + source
    outgoing_units = jnp.take(table, pick_index, axis=0).reshape(
        seq_count, 2, share_rows, local_width
    )
    arrived = lax.all_to_all(outgoing_units, SEQ, split_axis=0, concat_axis=2, tiled=True)
    merged = arrived.reshape(token_rows, local_width)
    full_rows = gathered_copies(merged, "head", 1)
    normed = rms_scale(full_rows.astype(jnp.float32), norm_gain).astype(jnp.bfloat16)
    model_width = in_proj.shape[0]
    head_count = head_decay_ceiling.shape[0]
    head_width = out_gain.shape[1]
    projected = jnp.dot(
        normed, in_proj.reshape(model_width, -1), preferred_element_type=jnp.float32
    )
    projected = projected.astype(jnp.bfloat16).reshape(token_rows, 4, head_count, head_width)
    gate_preactivation = jnp.dot(normed, decay_proj, preferred_element_type=jnp.float32)
    forget_element = jnp.where(
        unit_image == 1, jnp.log1p(-jnp.take(image_forget, jnp.take(image_here, my_units))), 0.0
    )
    start_offsets = jnp.arange(token_rows, dtype=jnp.int32) % patch_row_block == 0
    surge_logarithm = jnp.where(start_offsets, jnp.repeat(forget_element, patch_row_block), 0.0)
    decay_logarithm = (
        -head_decay_ceiling[None, :] * jax.nn.sigmoid(gate_preactivation) + surge_logarithm[:, None]
    )
    queries = projected[:, 0]
    key_rows = projected[:, 1]
    value_rows = projected[:, 2]
    gate_rows = projected[:, 3]
    within = jnp.cumsum(decay_logarithm, axis=0)
    span_decay = within[-1]
    scores = jnp.einsum("thd,shd->hts", queries, key_rows, preferred_element_type=jnp.float32)
    lagged = within.T[:, :, None] - within.T[:, None, :]
    row_ids = jnp.arange(token_rows, dtype=jnp.int32)
    causal = (row_ids[:, None] >= row_ids[None, :])[None]
    weights = jnp.where(causal, scores * jnp.exp(jnp.where(causal, lagged, 0.0)), 0.0).astype(
        jnp.bfloat16
    )
    inner_part = jnp.einsum("hts,shd->thd", weights, value_rows, preferred_element_type=jnp.float32)
    weighted_keys = key_rows.astype(jnp.float32) * jnp.exp(span_decay[None, :] - within)[:, :, None]
    local_state = jnp.einsum("thd,the->hde", weighted_keys, value_rows.astype(jnp.float32))

    def combine(earlier, later_part):
        return (
            earlier[0] + later_part[0],
            jnp.exp(later_part[0])[:, None, None] * earlier[1] + later_part[1],
        )

    identity = (jnp.zeros_like(span_decay), jnp.zeros_like(local_state))
    decay_before, entering = entering_2((span_decay, local_state), SEQ, combine, identity)
    carried = jnp.exp(within)[:, :, None] * jnp.einsum(
        "thd,hde->the", queries.astype(jnp.float32), entering
    )
    attended = inner_part + carried
    gated = rms_scale(attended, out_gain) * jax.nn.silu(gate_rows.astype(jnp.float32))
    gated = gated.astype(jnp.bfloat16).reshape(token_rows, -1)
    partial_out = jnp.dot(gated, out_proj, preferred_element_type=jnp.float32)
    summed = sent_and_summed_2(partial_out.astype(jnp.bfloat16), "head", 1)
    result = (merged.astype(jnp.float32) + summed).astype(jnp.bfloat16)
    result_shares = result.reshape(2, seq_count, share_rows, local_width)
    back_spread = lax.all_to_all(result_shares, SEQ, split_axis=1, concat_axis=1, tiled=True)
    back_table = back_spread.reshape(unit_count, share_rows, local_width)
    wanted = jnp.stack([unit_of_image, text_unit], axis=1).reshape(-1)
    back_index = wanted % 2 * seq_count + wanted // 2
    outgoing = jnp.take(back_table, back_index, axis=0).reshape(
        seq_count, 2, share_rows, local_width
    )
    returned = lax.all_to_all(outgoing, SEQ, split_axis=0, concat_axis=2, tiled=True)
    image_out = returned[:, 0]
    text_out = returned[0, 1]
    return (image_out, text_out)


def solution(mesh):
    split = Mesh(
        mesh.devices.reshape(4, 4, 2, mesh.shape["head"]), ("seq_0", "seq_1", "seq_2", "head")
    )
    return jax.shard_map(
        shards,
        mesh=split,
        in_specs=(
            P(SEQ, None, "head"),
            P(SEQ, "head"),
            P(),
            P(),
            P("head", None),
            P(),
            P(None, None, "head"),
            P(None, "head"),
            P("head"),
            P("head", None),
            P("head", None),
        ),
        out_specs=(P(SEQ, None, "head"), P(SEQ, "head")),
        check_vma=False,
    )
```

profile of v0, /device:TPU:1, one launch (start us, length us, event | category | flops | bytes accessed | tf_op | source)
XLA Modules:
  0.0 257.9 jit_solution(2699861484524103100)
XLA Ops:
  0.6 3.5 %convolution_bitcast_fusion = f32[4,256,512]{2,1,0:T(8,128)} fusion(bf16[36,4,8,512]{3,2,1,0:T(8,128)(2,1)} %bitcast.304, bf16[1,256,288]{1,2,0:T(8,128)(2,1)} %param.15), kind=kOutput, calls=%fused_computation.15 | convolution fusion | flops 301989888 | bytes 3424256 | tf_op jit(solution)/shard_map/dot_general | solution.py:113
  4.2 5.0 %all-to-all-start = ((f32[4,256,512]{2,1,0:T(8,128)}), f32[4,256,512]{2,1,0:T(8,128)}, u32[]{:S(2)}, u32[]{:S(2)}) async-start(f32[4,256,512]{2,1,0:T(8,128)} %convolution_bitcast_fusion), calls=%async_computation | async-start | bytes 4194304 | tf_op jit(solution)/shard_map/all_to_all | solution.py:19
  9.2 25.9 %all-to-all-done = f32[4,256,512]{2,1,0:T(8,128)} async-done(((f32[4,256,512]{2,1,0:T(8,128)}), f32[4,256,512]{2,1,0:T(8,128)}, u32[]{:S(2)}, u32[]{:S(2)}) %all-to-all-start) | async-done | bytes 2097184 | tf_op jit(solution)/shard_map/all_to_all | solution.py:19
  37.8 9.9 %all-to-all-start.1 = ((bf16[2,32,8,512]{3,2,0,1:T(8,128)(2,1)}), bf16[2,32,8,512]{3,2,0,1:T(8,128)(2,1)S(1)}, u32[]{:S(2)}, u32[]{:S(2)}) async-start(bf16[2,32,8,512]{3,2,0,1:T(8,128)(2,1)} %pad_maximum_fusion), calls=%async_computation.1 | async-start | bytes 1048576 | tf_op jit(solution)/shard_map/all_to_all | solution.py:116
  48.1 11.2 %all-to-all-done.1 = bf16[2,32,8,512]{3,2,0,1:T(8,128)(2,1)S(1)} async-done(((bf16[2,32,8,512]{3,2,0,1:T(8,128)(2,1)}), bf16[2,32,8,512]{3,2,0,1:T(8,128)(2,1)S(1)}, u32[]{:S(2)}, u32[]{:S(2)}) %all-to-all-start.1) | async-done | bytes 524320 | tf_op jit(solution)/shard_map/all_to_all | solution.py:116
  60.1 15.0 %all_to_all.58 = bf16[32,2,8,512]{3,2,1,0:T(8,128)(2,1)S(1)} all-to-all(bf16[32,2,8,512]{3,2,1,0:T(8,128)(2,1)S(1)} %bitcast.299), channel_id=1, replica_groups=mesh['seq_0'=4,'seq_1'=4,'seq_2'=2,'head'=4] {'seq_0','seq_1','seq_2'}, dimensions={0} | all-to-all | bytes 1048576 | tf_op jit(solution)/shard_map/all_to_all | solution.py:122
  78.7 4.8 %all-to-all-start.3 = ((bf16[4,512,512]{1,2,0:T(8,128)(2,1)}), bf16[4,512,512]{1,2,0:T(8,128)(2,1)}, u32[]{:S(2)}, u32[]{:S(2)}) async-start(bf16[4,512,512]{1,2,0:T(8,128)(2,1)} %broadcast_in_dim.53), calls=%async_computation.3 | async-start | bytes 4194304 | tf_op jit(solution)/shard_map/all_to_all | solution.py:31
  85.6 10.2 %copy.158 = bf16[256,8,4,512]{3,1,2,0:T(8,128)(2,1)} copy(bf16[256,8,4,512]{3,2,1,0:T(4,128)(2,1)} %bitcast.292) | data formatting | bytes 16777216
  96.6 13.5 %all-to-all-done.3 = bf16[4,512,512]{1,2,0:T(8,128)(2,1)} async-done(((bf16[4,512,512]{1,2,0:T(8,128)(2,1)}), bf16[4,512,512]{1,2,0:T(8,128)(2,1)}, u32[]{:S(2)}, u32[]{:S(2)}) %all-to-all-start.3) | async-done | bytes 2097184 | tf_op jit(solution)/shard_map/all_to_all | solution.py:31
  119.0 9.1 %convolution_convert_fusion.1 = bf16[512,2048]{1,0:T(8,128)(2,1)} fusion(bf16[512,2048]{0,1:T(8,128)(2,1)S(1)} %bitcast.303, bf16[2048,2048]{1,0:T(8,128)(2,1)} %bitcast.293), kind=kOutput, calls=%fused_computation.13 | convolution fusion | flops 4296015872 | bytes 12582912 | tf_op jit(solution)/shard_map/dot_general | solution.py:129
  128.1 4.4 %reshape.369 = bf16[512,4,4,128]{3,2,1,0:T(4,128)(2,1)} reshape(bf16[512,2048]{1,0:T(8,128)(2,1)} %convolution_convert_fusion.1) | data formatting | bytes 4194304 | tf_op jit(solution)/shard_map/reshape | solution.py:132
  132.6 3.2 %fusion.128 = (bf16[512,1,4,128]{3,2,1,0:T(4,128)(2,1)}, bf16[512,1,4,128]{3,2,1,0:T(4,128)(2,1)}, bf16[512,1,4,128]{3,2,1,0:T(4,128)(2,1)S(1)}, bf16[512,1,4,128]{3,2,1,0:T(4,128)(2,1)}) fusion(bf16[512,4,4,128]{3,2,1,0:T(4,128)(2,1)} %reshape.369), kind=kLoop, calls=%fused_computation.240 | loop fusion | bytes 4194304 | tf_op jit(solution)/shard_map/slice | solution.py:145
  138.8 2.2 all-gather
  143.0 9.9 %all_gather.31 = bf16[4,4,128,128]{3,2,1,0:T(8,128)(2,1)S(1)} all-gather(bf16[1,4,128,128]{3,2,1,0:T(8,128)(2,1)S(1)} %fusion.52), channel_id=1, replica_groups=mesh['seq_0'=4,'seq_1'=4,'seq_2'=2,'head'=4] {'seq_1'}, dimensions={0}, use_global_device_ids=true | all-gather | bytes 655360 | tf_op jit(solution)/shard_map/all_gather | solution.py:52
  152.9 6.5 %all-gather.2 = bf16[4,1,4]{2,1,0:T(2,128)(2,1)S(1)} all-gather(bf16[1,1,4]{2,1,0:T(2,128)(2,1)S(1)} %get-tuple-element.32), channel_id=1, replica_groups=mesh['seq_0'=4,'seq_1'=4,'seq_2'=2,'head'=4] {'seq_1'}, dimensions={0}, use_global_device_ids=true | all-gather | bytes 40 | tf_op jit(solution)/shard_map/all_gather | solution.py:52
  159.6 11.5 %all_gather.32 = bf16[4,4,128,128]{3,2,1,0:T(8,128)(2,1)} all-gather(bf16[1,4,128,128]{3,2,1,0:T(8,128)(2,1)S(1)} %fusion.46), channel_id=1, replica_groups=mesh['seq_0'=4,'seq_1'=4,'seq_2'=2,'head'=4] {'seq_0'}, dimensions={0}, use_global_device_ids=true | all-gather | bytes 655360 | tf_op jit(solution)/shard_map/all_gather | solution.py:52
  171.1 6.6 %all-gather.3 = bf16[4,1,4]{2,1,0:T(2,128)(2,1)S(1)} all-gather(bf16[1,1,4]{2,1,0:T(2,128)(2,1)S(1)} %get-tuple-element.26), channel_id=1, replica_groups=mesh['seq_0'=4,'seq_1'=4,'seq_2'=2,'head'=4] {'seq_0'}, dimensions={0}, use_global_device_ids=true | all-gather | bytes 40 | tf_op jit(solution)/shard_map/all_gather | solution.py:52
  177.7 4.4 %fusion.3 = f32[512,4,128]{0,2,1:T(8,128)} fusion(f32[4,512]{1,0:T(4,128)S(1)} %bitcast.310, pred[512,512]{1,0:T(8,128)(4,1)} %iota_compare_fusion, bf16[512,1,4,128]{0,3,2,1:T(8,128)(2,1)} %copy.152, bf16[512,1,4,128]{3,2,1,0:T(4,128)(2,1)} %get-tuple-element.13, bf16[512,1,4,128]{3,2,1,0:T(4,128)(2,1)} %get-tuple-element.15), kind=kOutput, calls=%fused_computation.17 | convolution fusion | flops 542113792 | bytes 2891776 | tf_op jit(solution)/shard_map/hts,shd->thd/dot_general | solution.py:155
  182.1 3.4 %multiply_reduce_fusion.1 = (f32[512,4]{0,1:T(4,128)S(1)}, f32[512,4,128]{0,2,1:T(8,128)}) fusion(f32[512,4,128]{0,2,1:T(8,128)} %fusion.3, bf16[512,1,4,128]{3,2,1,0:T(4,128)(2,1)} %get-tuple-element.13, bf16[4,4,128,128]{3,2,1,0:T(8,128)(2,1)} %all_gather.32, f32[4]{0:T(128)S(1)} %get-tuple-element.33, f32[4]{0:T(128)S(1)} %get-tuple-element.31, ...), kind=kOutput, calls=%fused_computation.39 | convolution fusion | flops 70842368 | bytes 3948746 | tf_op jit(solution)/shard_map/thd,hde->the/dot_general | solution.py:167
  191.2 4.4 %all-to-all-start.4 = ((bf16[4,512,512]{2,1,0:T(8,128)(2,1)}), bf16[4,512,512]{2,1,0:T(8,128)(2,1)}, u32[]{:S(2)}, u32[]{:S(2)}) async-start(bf16[4,512,512]{2,1,0:T(8,128)(2,1)} %bitcast.294), calls=%async_computation.4 | async-start | bytes 4194304 | tf_op jit(solution)/shard_map/all_to_all | solution.py:69
  195.7 16.7 %all-to-all-done.4 = bf16[4,512,512]{2,1,0:T(8,128)(2,1)} async-done(((bf16[4,512,512]{2,1,0:T(8,128)(2,1)}), bf16[4,512,512]{2,1,0:T(8,128)(2,1)}, u32[]{:S(2)}, u32[]{:S(2)}) %all-to-all-start.4) | async-done | bytes 2097184 | tf_op jit(solution)/shard_map/all_to_all | solution.py:69
  215.4 14.1 %all-to-all-start.5 = ((bf16[2,32,8,512]{3,2,0,1:T(8,128)(2,1)}), bf16[2,32,8,512]{3,2,0,1:T(8,128)(2,1)S(1)}, u32[]{:S(2)}, u32[]{:S(2)}) async-start(bf16[2,32,8,512]{3,2,0,1:T(8,128)(2,1)} %fusion.18), calls=%async_computation.5 | async-start | bytes 1048576 | tf_op jit(solution)/shard_map/all_to_all | solution.py:177
  229.9 11.3 %all-to-all-done.5 = bf16[2,32,8,512]{3,2,0,1:T(8,128)(2,1)S(1)} async-done(((bf16[2,32,8,512]{3,2,0,1:T(8,128)(2,1)}), bf16[2,32,8,512]{3,2,0,1:T(8,128)(2,1)S(1)}, u32[]{:S(2)}, u32[]{:S(2)}) %all-to-all-start.5) | async-done | bytes 524320 | tf_op jit(solution)/shard_map/all_to_all | solution.py:177
  242.0 15.0 %all_to_all.59 = bf16[32,2,8,512]{3,2,1,0:T(8,128)(2,1)S(1)} all-to-all(bf16[32,2,8,512]{3,2,1,0:T(8,128)(2,1)S(1)} %bitcast.301), channel_id=1, replica_groups=mesh['seq_0'=4,'seq_1'=4,'seq_2'=2,'head'=4] {'seq_0','seq_1','seq_2'}, dimensions={0} | all-to-all | bytes 1048576 | tf_op jit(solution)/shard_map/all_to_all | solution.py:184
  (90 shorter events, 35.1 us)
Async XLA Ops:
  0.6 187.8 %copy-start = (bf16[512,2048]{1,0:T(8,128)(2,1)S(1)}, bf16[512,2048]{1,0:T(8,128)(2,1)}, u32[]{:S(2)}) copy-start(bf16[512,2048]{1,0:T(8,128)(2,1)} %param.25) | copy-start | bytes 6291460
  4.2 5.0 %copy-start.7 = (s32[32]{0:T(128)S(1)}, s32[32]{0:T(128)}, u32[]{:S(2)}) copy-start(s32[32]{0:T(128)} %param.17) | copy-start | bytes 388
  4.2 30.9 %all-to-all-start = ((f32[4,256,512]{2,1,0:T(8,128)}), f32[4,256,512]{2,1,0:T(8,128)}, u32[]{:S(2)}, u32[]{:S(2)}) async-start(f32[4,256,512]{2,1,0:T(8,128)} %convolution_bitcast_fusion), calls=%async_computation | async-start | bytes 4194304 | tf_op jit(solution)/shard_map/all_to_all | solution.py:19
  9.1 27.8 %copy-start.2 = (bf16[256,512]{1,0:T(8,128)(2,1)S(1)}, bf16[256,512]{1,0:T(8,128)(2,1)}, u32[]{:S(2)}) copy-start(bf16[256,512]{1,0:T(8,128)(2,1)} %param.16) | copy-start | bytes 786436
  37.8 21.5 %all-to-all-start.1 = ((bf16[2,32,8,512]{3,2,0,1:T(8,128)(2,1)}), bf16[2,32,8,512]{3,2,0,1:T(8,128)(2,1)S(1)}, u32[]{:S(2)}, u32[]{:S(2)}) async-start(bf16[2,32,8,512]{3,2,0,1:T(8,128)(2,1)} %pad_maximum_fusion), calls=%async_computation.1 | async-start | bytes 1048576 | tf_op jit(solution)/shard_map/all_to_all | solution.py:116
  78.7 6.2 %copy-start.1 = (f32[32]{0:T(128)S(1)}, f32[32]{0:T(128)}, u32[]{:S(2)}) copy-start(f32[32]{0:T(128)} %param.18) | copy-start | bytes 388
  78.7 6.9 %copy-start.6 = (f32[4]{0:T(128)S(1)}, f32[4]{0:T(128)}, u32[]{:S(2)}) copy-start(f32[4]{0:T(128)} %param.23) | copy-start | bytes 52
  78.7 6.9 %copy-start.3 = (f32[2048]{0:T(1024)S(1)}, f32[2048]{0:T(1024)}, u32[]{:S(2)}) copy-start(f32[2048]{0:T(1024)} %param.20) | copy-start | bytes 24580
  78.7 31.4 %all-to-all-start.3 = ((bf16[4,512,512]{1,2,0:T(8,128)(2,1)}), bf16[4,512,512]{1,2,0:T(8,128)(2,1)}, u32[]{:S(2)}, u32[]{:S(2)}) async-start(bf16[4,512,512]{1,2,0:T(8,128)(2,1)} %broadcast_in_dim.53), calls=%async_computation.3 | async-start | bytes 4194304 | tf_op jit(solution)/shard_map/all_to_all | solution.py:31
  112.2 2.2 copy-start.4
  182.1 4.7 %copy-start.5 = (f32[4,128]{1,0:T(4,128)S(1)}, f32[4,128]{1,0:T(4,128)}, u32[]{:S(2)}) copy-start(f32[4,128]{1,0:T(4,128)} %param.24) | copy-start | bytes 6148
  191.2 21.2 %all-to-all-start.4 = ((bf16[4,512,512]{2,1,0:T(8,128)(2,1)}), bf16[4,512,512]{2,1,0:T(8,128)(2,1)}, u32[]{:S(2)}, u32[]{:S(2)}) async-start(bf16[4,512,512]{2,1,0:T(8,128)(2,1)} %bitcast.294), calls=%async_computation.4 | async-start | bytes 4194304 | tf_op jit(solution)/shard_map/all_to_all | solution.py:69
  215.4 25.8 %all-to-all-start.5 = ((bf16[2,32,8,512]{3,2,0,1:T(8,128)(2,1)}), bf16[2,32,8,512]{3,2,0,1:T(8,128)(2,1)S(1)}, u32[]{:S(2)}, u32[]{:S(2)}) async-start(bf16[2,32,8,512]{3,2,0,1:T(8,128)(2,1)} %fusion.18), calls=%async_computation.5 | async-start | bytes 1048576 | tf_op jit(solution)/shard_map/all_to_all | solution.py:177
where the time goes:
time: 259 us; the launch traced here: 258 us
  waiting for transfers between devices  78.7 us (30%)
  blocking collectives  68.5 us (26%)
  starting transfers between devices  38.2 us (15%)
  local copies, waits for them, and re-layouts  30.4 us (12%)
  matrix products  24 us (9%)
  other arithmetic  17.2 us (7%)
    all_gather x6, blocking collectives, entering_2(): lax.all_gather(part.astype(kind), axis)  38.5 us
    all_to_all x1, waiting for transfers between devices, sent_and_summed(): lax.all_to_all(pieces, axis, split_axis=0, concat_axis=0, tiled=True)  25.9 us
    all_to_all x1, waiting for transfers between devices, sent_and_summed_2(): lax.all_to_all(pieces, axis, split_axis=0, concat_axis=0, tiled=True)  16.7 us
    all_to_all x1, blocking collectives, shards(): lax.all_to_all(outgoing_units, SEQ, split_axis=0, concat_axis=2, tiled=True)  15 us
    all_to_all x1, blocking collectives, shards(): lax.all_to_all(outgoing, SEQ, split_axis=0, concat_axis=2, tiled=True)  15 us
    all_to_all x1, starting transfers between devices, shards(): lax.all_to_all(result_shares, SEQ, split_axis=1, concat_axis=1, tiled=True)  14.1 us
    all_to_all x1, waiting for transfers between devices, copy_for_each(): lax.all_to_all(jnp.broadcast_to(array[None], (length, *array.shape)), axi...  13.5 us
    unnamed x22, local copies, waits for them, and re-layouts  12.8 us
  transfers between devices with their start and end apart: 5, of which 5 were waited for; matrix products, arithmetic and copies ran while one was open for 5% of the time, Pallas kernels for 0%

commit v1 on v0

--- a/solution.py
+++ b/solution.py
@@ -113,7 +113,10 @@
     partial_value = jnp.dot(image_patches[0], adapter, preferred_element_type=jnp.float32)
     embedded = sent_and_summed(partial_value, "head", 1).astype(jnp.bfloat16)
     units_here = jnp.stack([embedded, text_embed]).reshape(2, seq_count, share_rows, local_width)
-    spread = lax.all_to_all(units_here, SEQ, split_axis=1, concat_axis=1, tiled=True)
+    spread = jnp.concatenate(
+        lax.all_to_all(jnp.stack(jnp.split(units_here, lax.axis_size(SEQ), axis=1)), SEQ, 0, 0),
+        axis=1,
+    )
     table = spread.reshape(unit_count, share_rows, local_width)
     pick_index = is_text * seq_count + source
     outgoing_units = jnp.take(table, pick_index, axis=0).reshape(

time: 259 us -> 278 us (1.073)
  other arithmetic: 17.2 us -> 34.8 us
    unnamed x1 -> x32, other arithmetic: 0.07 us -> 18.7 us
where the time goes in v1:
time: 278 us; the launch traced here: 276 us
  waiting for transfers between devices  78.7 us (28%)
  blocking collectives  68.5 us (25%)
  starting transfers between devices  38.2 us (14%)
  other arithmetic  34.8 us (13%)
  local copies, waits for them, and re-layouts  31.2 us (11%)
  matrix products  23.9 us (9%)
    all_gather x6, blocking collectives, entering_2(): lax.all_gather(part.astype(kind), axis)  38.5 us
    all_to_all x1, waiting for transfers between devices, sent_and_summed(): lax.all_to_all(pieces, axis, split_axis=0, concat_axis=0, tiled=True)  25.9 us
    unnamed x32, other arithmetic  18.7 us
    all_to_all x1, waiting for transfers between devices, sent_and_summed_2(): lax.all_to_all(pieces, axis, split_axis=0, concat_axis=0, tiled=True)  16.7 us
    all_to_all x1, blocking collectives, shards(): lax.all_to_all(outgoing_units, SEQ, split_axis=0, concat_axis=2, tiled=True)  15 us
    all_to_all x1, blocking collectives, shards(): lax.all_to_all(outgoing, SEQ, split_axis=0, concat_axis=2, tiled=True)  15 us
    all_to_all x1, starting transfers between devices, shards(): lax.all_to_all(result_shares, SEQ, split_axis=1, concat_axis=1, tiled=True)  14.1 us
    all_to_all x1, waiting for transfers between devices, copy_for_each(): lax.all_to_all(jnp.broadcast_to(array[None], (length, *array.shape)), axi...  13.5 us
  transfers between devices with their start and end apart: 5, of which 5 were waited for; matrix products, arithmetic and copies ran while one was open for 5% of the time, Pallas kernels for 0%

profile of v1, /device:TPU:1, one launch (start us, length us, event | category | flops | bytes accessed | tf_op | source)
XLA Modules:
  0.0 276.3 jit_solution(5406481574580685936)
XLA Ops:
  0.6 3.5 %convolution_bitcast_fusion = f32[4,256,512]{2,1,0:T(8,128)} fusion(bf16[36,4,8,512]{3,2,1,0:T(8,128)(2,1)} %bitcast.436, bf16[1,256,288]{1,2,0:T(8,128)(2,1)} %param.15), kind=kOutput, calls=%fused_computation.77 | convolution fusion | flops 301989888 | bytes 3424256 | tf_op jit(solution)/shard_map/dot_general | solution.py:113
  4.2 5.0 %all-to-all-start = ((f32[4,256,512]{2,1,0:T(8,128)}), f32[4,256,512]{2,1,0:T(8,128)}, u32[]{:S(2)}, u32[]{:S(2)}) async-start(f32[4,256,512]{2,1,0:T(8,128)} %convolution_bitcast_fusion), calls=%async_computation | async-start | bytes 4194304 | tf_op jit(solution)/shard_map/all_to_all | solution.py:19
  9.2 25.9 %all-to-all-done = f32[4,256,512]{2,1,0:T(8,128)} async-done(((f32[4,256,512]{2,1,0:T(8,128)}), f32[4,256,512]{2,1,0:T(8,128)}, u32[]{:S(2)}, u32[]{:S(2)}) %all-to-all-start) | async-done | bytes 2097184 | tf_op jit(solution)/shard_map/all_to_all | solution.py:19
  56.2 9.9 %all-to-all-start.1 = ((bf16[32,2,1,8,512]{4,3,1,2,0:T(8,128)(2,1)}), bf16[32,2,1,8,512]{4,3,1,2,0:T(8,128)(2,1)S(1)}, u32[]{:S(2)}, u32[]{:S(2)}) async-start(bf16[32,2,1,8,512]{4,3,1,2,0:T(8,128)(2,1)} %constant_dynamic-update-slice_fusion), calls=%async_computation.1 | async-start | bytes 1048576 | tf_op jit(solution)/shard_map/all_to_all | solution.py:117
  66.4 11.2 %all-to-all-done.1 = bf16[32,2,1,8,512]{4,3,1,2,0:T(8,128)(2,1)S(1)} async-done(((bf16[32,2,1,8,512]{4,3,1,2,0:T(8,128)(2,1)}), bf16[32,2,1,8,512]{4,3,1,2,0:T(8,128)(2,1)S(1)}, u32[]{:S(2)}, u32[]{:S(2)}) %all-to-all-start.1) | async-done | bytes 524320 | tf_op jit(solution)/shard_map/all_to_all | solution.py:117
  78.5 15.0 %all_to_all.58 = bf16[32,2,8,512]{3,2,1,0:T(8,128)(2,1)S(1)} all-to-all(bf16[32,2,8,512]{3,2,1,0:T(8,128)(2,1)S(1)} %bitcast.431), channel_id=1, replica_groups=mesh['seq_0'=4,'seq_1'=4,'seq_2'=2,'head'=4] {'seq_0','seq_1','seq_2'}, dimensions={0} | all-to-all | bytes 1048576 | tf_op jit(solution)/shard_map/all_to_all | solution.py:125
  97.0 4.8 %all-to-all-start.3 = ((bf16[4,512,512]{1,2,0:T(8,128)(2,1)}), bf16[4,512,512]{1,2,0:T(8,128)(2,1)}, u32[]{:S(2)}, u32[]{:S(2)}) async-start(bf16[4,512,512]{1,2,0:T(8,128)(2,1)} %broadcast_in_dim.53), calls=%async_computation.3 | async-start | bytes 4194304 | tf_op jit(solution)/shard_map/all_to_all | solution.py:31
  104.0 10.2 %copy.231 = bf16[256,8,4,512]{3,1,2,0:T(8,128)(2,1)} copy(bf16[256,8,4,512]{3,2,1,0:T(4,128)(2,1)} %bitcast.425) | data formatting | bytes 16777216
  115.0 13.5 %all-to-all-done.3 = bf16[4,512,512]{1,2,0:T(8,128)(2,1)} async-done(((bf16[4,512,512]{1,2,0:T(8,128)(2,1)}), bf16[4,512,512]{1,2,0:T(8,128)(2,1)}, u32[]{:S(2)}, u32[]{:S(2)}) %all-to-all-start.3) | async-done | bytes 2097184 | tf_op jit(solution)/shard_map/all_to_all | solution.py:31
  137.4 9.1 %convolution_convert_fusion.1 = bf16[512,2048]{1,0:T(8,128)(2,1)} fusion(bf16[512,2048]{0,1:T(8,128)(2,1)S(1)} %bitcast.435, bf16[2048,2048]{1,0:T(8,128)(2,1)} %bitcast.426), kind=kOutput, calls=%fused_computation.13 | convolution fusion | flops 4296015872 | bytes 12582912 | tf_op jit(solution)/shard_map/dot_general | solution.py:132
  146.5 4.4 %reshape.369 = bf16[512,4,4,128]{3,2,1,0:T(4,128)(2,1)} reshape(bf16[512,2048]{1,0:T(8,128)(2,1)} %convolution_convert_fusion.1) | data formatting | bytes 4194304 | tf_op jit(solution)/shard_map/reshape | solution.py:135
  150.9 3.2 %fusion.160 = (bf16[512,1,4,128]{3,2,1,0:T(4,128)(2,1)}, bf16[512,1,4,128]{3,2,1,0:T(4,128)(2,1)}, bf16[512,1,4,128]{3,2,1,0:T(4,128)(2,1)S(1)}, bf16[512,1,4,128]{3,2,1,0:T(4,128)(2,1)}) fusion(bf16[512,4,4,128]{3,2,1,0:T(4,128)(2,1)} %reshape.369), kind=kLoop, calls=%fused_computation.366 | loop fusion | bytes 4194304 | tf_op jit(solution)/shard_map/slice | solution.py:148
  157.2 2.2 all-gather
  161.4 9.9 %all_gather.31 = bf16[4,4,128,128]{3,2,1,0:T(8,128)(2,1)S(1)} all-gather(bf16[1,4,128,128]{3,2,1,0:T(8,128)(2,1)S(1)} %fusion.52), channel_id=1, replica_groups=mesh['seq_0'=4,'seq_1'=4,'seq_2'=2,'head'=4] {'seq_1'}, dimensions={0}, use_global_device_ids=true | all-gather | bytes 655360 | tf_op jit(solution)/shard_map/all_gather | solution.py:52
  171.3 6.5 %all-gather.2 = bf16[4,1,4]{2,1,0:T(2,128)(2,1)S(1)} all-gather(bf16[1,1,4]{2,1,0:T(2,128)(2,1)S(1)} %get-tuple-element.32), channel_id=1, replica_groups=mesh['seq_0'=4,'seq_1'=4,'seq_2'=2,'head'=4] {'seq_1'}, dimensions={0}, use_global_device_ids=true | all-gather | bytes 40 | tf_op jit(solution)/shard_map/all_gather | solution.py:52
  177.9 11.5 %all_gather.32 = bf16[4,4,128,128]{3,2,1,0:T(8,128)(2,1)} all-gather(bf16[1,4,128,128]{3,2,1,0:T(8,128)(2,1)S(1)} %fusion.46), channel_id=1, replica_groups=mesh['seq_0'=4,'seq_1'=4,'seq_2'=2,'head'=4] {'seq_0'}, dimensions={0}, use_global_device_ids=true | all-gather | bytes 655360 | tf_op jit(solution)/shard_map/all_gather | solution.py:52
  189.5 6.6 %all-gather.3 = bf16[4,1,4]{2,1,0:T(2,128)(2,1)S(1)} all-gather(bf16[1,1,4]{2,1,0:T(2,128)(2,1)S(1)} %get-tuple-element.26), channel_id=1, replica_groups=mesh['seq_0'=4,'seq_1'=4,'seq_2'=2,'head'=4] {'seq_0'}, dimensions={0}, use_global_device_ids=true | all-gather | bytes 40 | tf_op jit(solution)/shard_map/all_gather | solution.py:52
  196.1 4.3 %fusion.3 = f32[512,4,128]{0,2,1:T(8,128)} fusion(f32[4,512]{1,0:T(4,128)S(1)} %bitcast.440, pred[512,512]{1,0:T(8,128)(4,1)} %iota_compare_fusion, bf16[512,1,4,128]{0,3,2,1:T(8,128)(2,1)} %copy.225, bf16[512,1,4,128]{3,2,1,0:T(4,128)(2,1)} %get-tuple-element.13, bf16[512,1,4,128]{3,2,1,0:T(4,128)(2,1)} %get-tuple-element.15), kind=kOutput, calls=%fused_computation.79 | convolution fusion | flops 542113792 | bytes 2891776 | tf_op jit(solution)/shard_map/hts,shd->thd/dot_general | solution.py:158
  200.4 3.4 %multiply_reduce_fusion.1 = (f32[512,4]{0,1:T(4,128)S(1)}, f32[512,4,128]{0,2,1:T(8,128)}) fusion(f32[512,4,128]{0,2,1:T(8,128)} %fusion.3, bf16[512,1,4,128]{3,2,1,0:T(4,128)(2,1)} %get-tuple-element.13, bf16[4,4,128,128]{3,2,1,0:T(8,128)(2,1)} %all_gather.32, f32[4]{0:T(128)S(1)} %get-tuple-element.33, f32[4]{0:T(128)S(1)} %get-tuple-element.31, ...), kind=kOutput, calls=%fused_computation.101 | convolution fusion | flops 70842368 | bytes 3948746 | tf_op jit(solution)/shard_map/thd,hde->the/dot_general | solution.py:170
  209.6 4.4 %all-to-all-start.4 = ((bf16[4,512,512]{2,1,0:T(8,128)(2,1)}), bf16[4,512,512]{2,1,0:T(8,128)(2,1)}, u32[]{:S(2)}, u32[]{:S(2)}) async-start(bf16[4,512,512]{2,1,0:T(8,128)(2,1)} %bitcast.427), calls=%async_computation.4 | async-start | bytes 4194304 | tf_op jit(solution)/shard_map/all_to_all | solution.py:69
  214.0 16.7 %all-to-all-done.4 = bf16[4,512,512]{2,1,0:T(8,128)(2,1)} async-done(((bf16[4,512,512]{2,1,0:T(8,128)(2,1)}), bf16[4,512,512]{2,1,0:T(8,128)(2,1)}, u32[]{:S(2)}, u32[]{:S(2)}) %all-to-all-start.4) | async-done | bytes 2097184 | tf_op jit(solution)/shard_map/all_to_all | solution.py:69
  233.8 14.1 %all-to-all-start.5 = ((bf16[2,32,8,512]{3,2,0,1:T(8,128)(2,1)}), bf16[2,32,8,512]{3,2,0,1:T(8,128)(2,1)S(1)}, u32[]{:S(2)}, u32[]{:S(2)}) async-start(bf16[2,32,8,512]{3,2,0,1:T(8,128)(2,1)} %copy.219), calls=%async_computation.5 | async-start | bytes 1048576 | tf_op jit(solution)/shard_map/all_to_all | solution.py:180
  248.3 11.3 %all-to-all-done.5 = bf16[2,32,8,512]{3,2,0,1:T(8,128)(2,1)S(1)} async-done(((bf16[2,32,8,512]{3,2,0,1:T(8,128)(2,1)}), bf16[2,32,8,512]{3,2,0,1:T(8,128)(2,1)S(1)}, u32[]{:S(2)}, u32[]{:S(2)}) %all-to-all-start.5) | async-done | bytes 524320 | tf_op jit(solution)/shard_map/all_to_all | solution.py:180
  260.5 15.0 %all_to_all.59 = bf16[32,2,8,512]{3,2,1,0:T(8,128)(2,1)S(1)} all-to-all(bf16[32,2,8,512]{3,2,1,0:T(8,128)(2,1)S(1)} %bitcast.433), channel_id=1, replica_groups=mesh['seq_0'=4,'seq_1'=4,'seq_2'=2,'head'=4] {'seq_0','seq_1','seq_2'}, dimensions={0} | all-to-all | bytes 1048576 | tf_op jit(solution)/shard_map/all_to_all | solution.py:187
  (122 shorter events, 53.5 us)
Async XLA Ops:
  0.6 206.1 %copy-start = (bf16[512,2048]{1,0:T(8,128)(2,1)S(1)}, bf16[512,2048]{1,0:T(8,128)(2,1)}, u32[]{:S(2)}) copy-start(bf16[512,2048]{1,0:T(8,128)(2,1)} %param.25) | copy-start | bytes 6291460
  4.2 5.0 %copy-start.7 = (s32[32]{0:T(128)S(1)}, s32[32]{0:T(128)}, u32[]{:S(2)}) copy-start(s32[32]{0:T(128)} %param.17) | copy-start | bytes 388
  4.2 30.9 %all-to-all-start = ((f32[4,256,512]{2,1,0:T(8,128)}), f32[4,256,512]{2,1,0:T(8,128)}, u32[]{:S(2)}, u32[]{:S(2)}) async-start(f32[4,256,512]{2,1,0:T(8,128)} %convolution_bitcast_fusion), calls=%async_computation | async-start | bytes 4194304 | tf_op jit(solution)/shard_map/all_to_all | solution.py:19
  9.1 27.8 %copy-start.2 = (bf16[256,512]{1,0:T(8,128)(2,1)S(1)}, bf16[256,512]{1,0:T(8,128)(2,1)}, u32[]{:S(2)}) copy-start(bf16[256,512]{1,0:T(8,128)(2,1)} %param.16) | copy-start | bytes 786436
  56.2 21.5 %all-to-all-start.1 = ((bf16[32,2,1,8,512]{4,3,1,2,0:T(8,128)(2,1)}), bf16[32,2,1,8,512]{4,3,1,2,0:T(8,128)(2,1)S(1)}, u32[]{:S(2)}, u32[]{:S(2)}) async-start(bf16[32,2,1,8,512]{4,3,1,2,0:T(8,128)(2,1)} %constant_dynamic-update-slice_fusion), calls=%async_computation.1 | async-start | bytes 1048576 | tf_op jit(solution)/shard_map/all_to_all | solution.py:117
  97.0 6.2 %copy-start.1 = (f32[32]{0:T(128)S(1)}, f32[32]{0:T(128)}, u32[]{:S(2)}) copy-start(f32[32]{0:T(128)} %param.18) | copy-start | bytes 388
  97.0 6.9 %copy-start.6 = (f32[4]{0:T(128)S(1)}, f32[4]{0:T(128)}, u32[]{:S(2)}) copy-start(f32[4]{0:T(128)} %param.23) | copy-start | bytes 52
  97.0 6.9 %copy-start.3 = (f32[2048]{0:T(1024)S(1)}, f32[2048]{0:T(1024)}, u32[]{:S(2)}) copy-start(f32[2048]{0:T(1024)} %param.20) | copy-start | bytes 24580
  97.0 31.4 %all-to-all-start.3 = ((bf16[4,512,512]{1,2,0:T(8,128)(2,1)}), bf16[4,512,512]{1,2,0:T(8,128)(2,1)}, u32[]{:S(2)}, u32[]{:S(2)}) async-start(bf16[4,512,512]{1,2,0:T(8,128)(2,1)} %broadcast_in_dim.53), calls=%async_computation.3 | async-start | bytes 4194304 | tf_op jit(solution)/shard_map/all_to_all | solution.py:31
  130.6 2.2 copy-start.4
  200.4 4.7 %copy-start.5 = (f32[4,128]{1,0:T(4,128)S(1)}, f32[4,128]{1,0:T(4,128)}, u32[]{:S(2)}) copy-start(f32[4,128]{1,0:T(4,128)} %param.24) | copy-start | bytes 6148
  209.6 21.2 %all-to-all-start.4 = ((bf16[4,512,512]{2,1,0:T(8,128)(2,1)}), bf16[4,512,512]{2,1,0:T(8,128)(2,1)}, u32[]{:S(2)}, u32[]{:S(2)}) async-start(bf16[4,512,512]{2,1,0:T(8,128)(2,1)} %bitcast.427), calls=%async_computation.4 | async-start | bytes 4194304 | tf_op jit(solution)/shard_map/all_to_all | solution.py:69
  233.8 25.8 %all-to-all-start.5 = ((bf16[2,32,8,512]{3,2,0,1:T(8,128)(2,1)}), bf16[2,32,8,512]{3,2,0,1:T(8,128)(2,1)S(1)}, u32[]{:S(2)}, u32[]{:S(2)}) async-start(bf16[2,32,8,512]{3,2,0,1:T(8,128)(2,1)} %copy.219), calls=%async_computation.5 | async-start | bytes 1048576 | tf_op jit(solution)/shard_map/all_to_all | solution.py:180
